TPU v7x, 32 devices: a whole 2x2x4 slice. The times are simulated.
32 devices in a mesh: site: 4 (over y, x), bond: 8 (over z, core).
Axes of the slice: x: 2, y: 2, z: 4, core: 2. Of those that a mesh axis runs over, the one named last changes fastest.
Arguments:
- start_rows: bfloat16 [1024, 4096], P(None, 'bond'), may hold values from -6 to 6
- site_tensors: bfloat16 [4, 4096, 8, 4096], P('site', None, None, 'bond'), may hold values from -0.09375 to 0.09375
- block_scales: float32 [4, 8, 32], P('site', None, 'bond'), may hold values from 0.25 to 1
- displacement: float32 [4, 8, 8], P('site'), may hold values from -0.9 to 0.9
- outcomes: int32 [4, 1024], P('site'), may hold values from 0 to 7
Outputs:
- leaving: bfloat16 [4, 1024, 4096], P('site', None, 'bond')
- log_norms: float32 [4, 1024], P('site')
Inputs may be any that keep to these rules, and one draw needn't show every extreme that they name: outcomes index the second dimension of displacement.
All inputs are finite; a program needn't handle non-finite values.
Results may differ from a plain program's by a relative error of at most 0.014.
Values may be sent and summed in bfloat16 or wider, within the bound.
A program may use at most 128 MiB of HBM per device.

v0:
```python
import functools
import jax
import jax.numpy as jnp
from jax import lax
from jax.experimental import pallas as pl
from jax.experimental.pallas import tpu as pltpu
from jax.sharding import PartitionSpec as P

ROWS = 128
CHUNK = 32
SLOTS = 8
LANES = 128
MESH = pl.DeviceIdType.MESH


def kernel(sites, bond, start_hbm, tensor_hbm, scale_ref, weight_ref, leave_ref, log_ref,
           mats, gathered, landing, wide, total,
           start_sem, load_sem, send_up, send_down, send_pair, send_site,
           recv_line, recv_pair, recv_site):
    chi, phys, cols = tensor_hbm.shape
    allrows = leave_ref.shape[0]
    rows = min(ROWS, allrows)
    batches = allrows // rows
    chips = bond // 2
    site = lax.axis_index("site")
    me = lax.axis_index("bond")
    chip = me // 2
    core = me % 2
    pair = me + 1 - 2 * core
    has_up = chip < chips - 1
    has_down = chip > 0
    first_site = site == 0
    has_next = site < sites - 1

    def block(ref, b, owner):
        return ref.at[pl.ds(pl.multiple_of(b * rows, rows), rows),
                      pl.ds(pl.multiple_of(owner * cols, cols), cols)]

    def up_copy(b, source):
        piece = block(gathered, b, 2 * source + core)
        return pltpu.make_async_remote_copy(
            piece, piece, send_up.at[b, source], recv_line.at[b, source],
            device_id={"bond": me + 2}, device_id_type=MESH)

    def down_copy(b, source):
        piece = block(gathered, b, 2 * source + core)
        return pltpu.make_async_remote_copy(
            piece, piece, send_down.at[b, source], recv_line.at[b, source],
            device_id={"bond": me - 2}, device_id_type=MESH)

    def pair_copy(b, source):
        piece = block(gathered, b, 2 * source + core)
        return pltpu.make_async_remote_copy(
            piece, piece, send_pair.at[b, source], recv_pair.at[b, source],
            device_id={"bond": pair}, device_id_type=MESH)

    def site_copy(b):
        return pltpu.make_async_remote_copy(
            leave_ref.at[pl.ds(pl.multiple_of(b * rows, rows), rows), :],
            block(gathered, b, me), send_site.at[b], recv_site.at[b],
            device_id={"site": site + 1}, device_id_type=MESH)

    def arrived_line(b, source):
        piece = block(gathered, b, 2 * source + core)
        pltpu.make_async_remote_copy(
            piece, piece, send_up.at[b, source], recv_line.at[b, source],
            device_id={"bond": pair}, device_id_type=MESH).wait_recv()

    def arrived_pair(b, source):
        piece = block(gathered, b, 2 * source + 1 - core)
        pltpu.make_async_remote_copy(
            piece, piece, send_pair.at[b, source], recv_pair.at[b, source],
            device_id={"bond": pair}, device_id_type=MESH).wait_recv()

    def relay(b, hop):
        if hop == 0:
            @pl.when(jnp.logical_not(first_site))
            def _():
                piece = block(gathered, b, me)
                pltpu.make_async_remote_copy(
                    piece, piece, send_site.at[b], recv_site.at[b],
                    device_id={"bond": pair}, device_id_type=MESH).wait_recv()

            @pl.when(has_up)
            def _():
                up_copy(b, chip).start()

            @pl.when(has_down)
            def _():
                down_copy(b, chip).start()

            pair_copy(b, chip).start()
            return

        @pl.when(chip - hop >= 0)
        def _():
            arrived_line(b, chip - hop)

            @pl.when(has_up)
            def _():
                up_copy(b, chip - hop).start()

            pair_copy(b, chip - hop).start()

        @pl.when(chip + hop < chips)
        def _():
            arrived_line(b, chip + hop)

            @pl.when(has_down)
            def _():
                down_copy(b, chip + hop).start()

            pair_copy(b, chip + hop).start()

    def load(step, slot):
        return pltpu.make_async_copy(
            tensor_hbm.at[pl.ds(pl.multiple_of(step * CHUNK, CHUNK), CHUNK)],
            landing.at[slot], load_sem.at[slot])

    steps = chi // CHUNK
    for step in range(SLOTS):
        load(step, step).start()

    @pl.when(first_site)
    def _():
        pltpu.make_async_copy(
            start_hbm, gathered.at[:, pl.ds(pl.multiple_of(me * cols, cols), cols)],
            start_sem).start()

    barrier = pltpu.get_barrier_semaphore()

    def greet(there, device):
        @pl.when(there)
        def _():
            pl.semaphore_signal(barrier, inc=1, device_id=device, device_id_type=MESH)

    around = ((has_up, {"bond": me + 2}), (has_down, {"bond": me - 2}),
              (chip >= 0, {"bond": pair}),
              (has_next, {"site": site + 1}), (site > 0, {"site": site - 1}))
    for there, device in around:
        greet(there, device)
    peers = sum(there.astype(jnp.int32) for there, _ in around)
    pl.semaphore_wait(barrier, peers)

    @pl.when(first_site)
    def _():
        pltpu.make_async_copy(
            start_hbm, gathered.at[:, pl.ds(pl.multiple_of(me * cols, cols), cols)],
            start_sem).wait()

    def spread(step, carry):
        slot = lax.rem(step, SLOTS)
        load(step, slot).wait()
        for t in range(cols // LANES):
            strip = slice(t * LANES, (t + 1) * LANES)
            wide[t] = landing[slot, :, :, strip].astype(jnp.float32).reshape(CHUNK * phys, LANES)
            for p in range(phys):
                mats[p, pl.ds(pl.multiple_of(step * CHUNK, CHUNK), CHUNK), strip] = (
                    wide[t, pl.ds(p, CHUNK, stride=phys), :].astype(jnp.bfloat16))

        @pl.when(step + SLOTS < steps)
        def _():
            load(step + SLOTS, slot).start()
        return carry

    for part in range(chips):
        @pl.when(first_site)
        def _():
            relay(0, part)
        lax.fori_loop(part * steps // chips, (part + 1) * steps // chips, spread, 0)

    @pl.when(jnp.logical_not(first_site))
    def _():
        for part in range(chips):
            relay(0, part)

    def batch(b, carry):
        for source in range(chips):
            arrived_pair(b, source)
        here = pl.ds(pl.multiple_of(b * rows, rows), rows)
        squares = jnp.zeros((rows, LANES), jnp.float32)
        for t in range(chi // LANES):
            x = gathered[here, t * LANES:(t + 1) * LANES].astype(jnp.float32)
            squares = squares + x * x
        norm = jnp.sqrt(jnp.sum(squares, axis=1, keepdims=True) / chi + 1e-06)
        log_ref[here, :] = jnp.log(norm)
        for p in range(phys):
            @pl.when(b + 1 < batches)
            def _():
                if p == 0:
                    relay(b + 1, 0)
                if p == phys - 1 and chips > 1:
                    relay(b + 1, 1)
            prod = jnp.dot(gathered[here, :], mats[p], preferred_element_type=jnp.float32)
            prod = prod * scale_ref[p:p + 1, :] * weight_ref[here, p:p + 1]
            if p == 0:
                total[...] = prod
            elif p < phys - 1:
                total[...] += prod
            else:
                leave_ref[here, :] = ((total[...] + prod) / norm).astype(jnp.bfloat16)

        @pl.when(has_next)
        def _():
            site_copy(b).start()

        @pl.when(b + 1 < batches)
        def _():
            for part in range(2, chips):
                relay(b + 1, part)
        return carry

    lax.fori_loop(0, batches, batch, 0)

    def drain(b, carry):
        @pl.when(has_next)
        def _():
            site_copy(b).wait_send()
        for source in range(chips):
            pair_copy(b, source).wait_send()

            @pl.when(jnp.logical_and(has_up, source <= chip))
            def _():
                up_copy(b, source).wait_send()

            @pl.when(jnp.logical_and(has_down, source >= chip))
            def _():
                down_copy(b, source).wait_send()
        return carry

    lax.fori_loop(0, batches, drain, 0)


def local(start_rows, site_tensors, block_scales, displacement, outcomes):
    sites = lax.axis_size("site")
    bond = lax.axis_size("bond")
    _, chi, phys, cols = site_tensors.shape
    allrows = start_rows.shape[0]
    nblk = block_scales.shape[2]
    scales = jnp.repeat(block_scales[0], cols // nblk, axis=1)
    onehot = (outcomes[0][:, None] == jnp.arange(phys, dtype=jnp.int32)[None, :]).astype(jnp.float32)
    weight = jnp.sum(onehot[:, :, None] * displacement[0][None], axis=1)
    batches = allrows // min(ROWS, allrows)
    chips = bond // 2
    sems = pltpu.SemaphoreType.DMA
    leave, logs = pl.pallas_call(
        functools.partial(kernel, sites, bond),
        out_shape=(jax.ShapeDtypeStruct((allrows, cols), jnp.bfloat16),
                   jax.ShapeDtypeStruct((allrows, 1), jnp.float32)),
        in_specs=[pl.BlockSpec(memory_space=pl.ANY), pl.BlockSpec(memory_space=pl.ANY),
                  pl.BlockSpec(memory_space=pltpu.VMEM), pl.BlockSpec(memory_space=pltpu.VMEM)],
        out_specs=(pl.BlockSpec(memory_space=pltpu.VMEM), pl.BlockSpec(memory_space=pltpu.VMEM)),
        scratch_shapes=[
            pltpu.VMEM((phys, chi, cols), jnp.bfloat16),
            pltpu.VMEM((allrows, chi), jnp.bfloat16),
            pltpu.VMEM((SLOTS, CHUNK, phys, cols), jnp.bfloat16),
            pltpu.VMEM((cols // LANES, CHUNK * phys, LANES), jnp.float32),
            pltpu.VMEM((min(ROWS, allrows), cols), jnp.float32),
            sems(()), sems((SLOTS,)),
            sems((batches, chips)), sems((batches, chips)), sems((batches, chips)), sems((batches,)),
            sems((batches, chips)), sems((batches, chips)), sems((batches,)),
        ],
        compiler_params=pltpu.CompilerParams(
            collective_id=0, has_side_effects=True, vmem_limit_bytes=64000000),
    )(start_rows, site_tensors[0], scales, weight)
    return leave[None], logs[:, 0][None]


def solution(mesh):
    return jax.shard_map(
        local,
        mesh=mesh,
        in_specs=(
            P(None, "bond"),
            P("site", None, None, "bond"),
            P("site", None, "bond"),
            P("site", None, None),
            P("site", None),
        ),
        out_specs=(P("site", None, "bond"), P("site", None)),
        check_vma=False,
    )
```

profile of v0, /device:TPU:7, one launch (start us, length us, event | category | flops | bytes accessed | tf_op | source)
XLA Modules:
  0.0 218.3 jit_solution(11566502416462440546)
XLA Ops:
  0.6 0.0 copy-start
  0.6 0.7 copy-done
  1.3 0.7 broadcast_bitcast_fusion.scale_ref
  2.0 0.7 fusion
  2.7 0.8 multiply_reduce_fusion
  3.5 1.0 copy.7.weight_ref
  4.5 209.7 %shard_map.68 = (bf16[1024,512]{1,0:T(8,128)(2,1)}, f32[1024,1]{1,0:T(8,128)}) custom-call(bf16[1024,512]{1,0:T(8,128)(2,1)} %start_hbm.1, bf16[4096,8,512]{2,1,0:T(8,128)(2,1)} %bitcast.9, f32[8,512]{1,0:T(8,128)} %broadcast_bitcast_fusion.scale_ref, f32[1024,8]{1,0:T(8,128)} %copy.7.weight_ref), custom_call_target="tpu_custom_call" | custom-call | tf_op jit(solution)/shard_map/pallas_call | solution.py:246
  214.2 1.8 reduce
  216.0 2.3 %copy.9 = bf16[1,1024,512]{2,1,0:T(8,128)(2,1)} copy(bf16[1,1024,512]{2,1,0:T(8,128)(2,1)} %bitcast.10) | data formatting | bytes 2097152
Async XLA Ops:
  0.6 0.7 copy-start
where the time goes:
time: 219 us; the launch traced here: 218 us
  Pallas kernels  210 us (96%)
  local copies, waits for them, and re-layouts  4.61 us (2%)
  other arithmetic  3.31 us (2%)
    pallas_call x1, Pallas kernels, local(): pl.pallas_call(functools.partial(kernel, sites, bond), out_shape=(jax.Sha...  210 us

commit v1 on v0

v1 whole, which is shorter than its diff:
```python
import functools
import jax
import jax.numpy as jnp
from jax import lax
from jax.experimental import pallas as pl
from jax.experimental.pallas import tpu as pltpu
from jax.sharding import PartitionSpec as P

ROWS = 128
PIECES = 2
CHUNK = 64
SLOTS = 8
LANES = 128
MESH = pl.DeviceIdType.MESH


def kernel(sites, bond, start_hbm, tensor_hbm, scale_ref, disp_ref, outcome_ref, leave_ref, log_ref,
           mats, gathered, landing, wide, total, squares, weight_ref, scales,
           start_sem, load_sem, send_up, send_down, send_pair, send_site,
           recv_line, recv_pair, recv_site):
    chi, phys, cols = tensor_hbm.shape
    allrows = leave_ref.shape[0]
    rows = min(ROWS, allrows)
    piece = rows // PIECES
    batches = allrows // rows
    chips = bond // 2
    wide_cols = 2 * cols
    chunk = min(CHUNK, wide_cols)
    site = lax.axis_index("site")
    me = lax.axis_index("bond")
    chip = me // 2
    core = me % 2
    pair = me + 1 - 2 * core
    has_up = chip < chips - 1
    has_down = chip > 0
    at_end = jnp.logical_or(chip == 0, chip == chips - 1)
    first_site = site == 0
    later_site = site > 0
    has_next = site < sites - 1

    low_half = chip < chips - 1 - chip
    spread_of = jnp.minimum(chip, chips - 1 - chip)

    def source_of(j):
        if j == 0:
            return chip
        near = chip - (j + 1) // 2 if j % 2 else chip + j // 2
        far = jnp.where(low_half, j, chips - 1 - j)
        return jnp.where(j <= 2 * spread_of, near, far)

    def block(q, source, lane_core):
        return gathered.at[source, pl.ds(pl.multiple_of(q * piece, piece), piece),
                           pl.ds(pl.multiple_of(lane_core * cols, cols), cols)]

    def line_copy(q, source, sem, to):
        ref = block(q, source, core)
        return pltpu.make_async_remote_copy(
            ref, ref, sem.at[q, source], recv_line.at[q, source],
            device_id={"bond": to}, device_id_type=MESH)

    def up_copy(q, source):
        return line_copy(q, source, send_up, me + 2)

    def down_copy(q, source):
        return line_copy(q, source, send_down, me - 2)

    def pair_copy(q, source, lane_core):
        ref = block(q, source, lane_core)
        return pltpu.make_async_remote_copy(
            ref, ref, send_pair.at[q, source], recv_pair.at[q, source],
            device_id={"bond": pair}, device_id_type=MESH)

    def site_copy(q):
        return pltpu.make_async_remote_copy(
            leave_ref.at[pl.ds(pl.multiple_of(q * piece, piece), piece), :],
            block(q, chip, core), send_site.at[q], recv_site.at[q],
            device_id={"site": site + 1}, device_id_type=MESH)

    def own(q):
        @pl.when(later_site)
        def _():
            ref = block(q, chip, core)
            pltpu.make_async_remote_copy(
                ref, ref, send_site.at[q], recv_site.at[q],
                device_id={"bond": pair}, device_id_type=MESH).wait_recv()

        @pl.when(has_down)
        def _():
            down_copy(q, chip).start()

        @pl.when(has_up)
        def _():
            up_copy(q, chip).start()

        pair_copy(q, chip, core).start()

    def arrive(q, hop):
        @pl.when(chip - hop >= 0)
        def _():
            line_copy(q, chip - hop, send_up, pair).wait_recv()

            @pl.when(has_up)
            def _():
                up_copy(q, chip - hop).start()

            pair_copy(q, chip - hop, core).start()

        @pl.when(chip + hop < chips)
        def _():
            line_copy(q, chip + hop, send_down, pair).wait_recv()

            @pl.when(has_down)
            def _():
                down_copy(q, chip + hop).start()

            pair_copy(q, chip + hop, core).start()

    per_source = wide_cols // chunk

    def load(j, i, slot):
        base = source_of(j) * wide_cols + i * chunk
        return pltpu.make_async_copy(
            tensor_hbm.at[pl.ds(pl.multiple_of(base, chunk), chunk)],
            landing.at[slot], load_sem.at[slot])

    start_copy = pltpu.make_async_copy(
        start_hbm, gathered.at[chip, :, pl.ds(pl.multiple_of(core * cols, cols), cols)], start_sem)

    @pl.when(first_site)
    def _():
        start_copy.start()

    slots = min(SLOTS, per_source)
    for step in range(slots):
        load(0, step, step).start()

    barrier = pltpu.get_barrier_semaphore()

    def greet(there, device):
        @pl.when(there)
        def _():
            pl.semaphore_signal(barrier, inc=1, device_id=device, device_id_type=MESH)

    around = ((has_up, {"bond": me + 2}), (has_down, {"bond": me - 2}),
              (chip >= 0, {"bond": pair}),
              (has_next, {"site": site + 1}), (later_site, {"site": site - 1}))
    for there, device in around:
        greet(there, device)
    peers = sum(there.astype(jnp.int32) for there, _ in around)
    pl.semaphore_wait(barrier, peers)

    @pl.when(first_site)
    def _():
        start_copy.wait()
        for h in range(PIECES):
            own(h)

    nblk = scale_ref.shape[0]
    width = cols // nblk
    for p in range(phys):
        for n in range(nblk):
            scales[p:p + 1, n * width:(n + 1) * width] = jnp.full((1, width), scale_ref[n, p], jnp.float32)
    for b in range(batches):
        row = outcome_ref[0:1, b * rows:(b + 1) * rows]
        column = jnp.transpose(jnp.broadcast_to(row, (rows, rows)))[:, :phys]
        weight = jnp.zeros((rows, phys), jnp.float32)
        for o in range(phys):
            weight = jnp.where(column == o, disp_ref[o:o + 1, :], weight)
        weight_ref[b * rows:(b + 1) * rows, :] = weight

    def spread(j):
        source = source_of(j)

        def step(i, carry):
            slot = lax.rem(i, slots)
            load(j, i, slot).wait()
            for t in range(cols // LANES):
                strip = slice(t * LANES, (t + 1) * LANES)
                wide[t] = landing[slot, :, :, strip].astype(jnp.float32).reshape(chunk * phys, LANES)
                for p in range(phys):
                    mats[p, source, pl.ds(pl.multiple_of(i * chunk, chunk), chunk), strip] = (
                        wide[t, pl.ds(p, chunk, stride=phys), :].astype(jnp.bfloat16))

            @pl.when(i + slots < per_source)
            def _():
                load(j, i + slots, slot).start()

            if j + 1 < chips:
                @pl.when(i + slots >= per_source)
                def _():
                    load(j + 1, i + slots - per_source, slot).start()
            return carry

        lax.fori_loop(0, per_source, step, 0)

    @pl.when(later_site)
    def _():
        for j in range(chips):
            spread(j)
        for h in range(PIECES):
            own(h)

    half = phys // 2

    def batch(b, carry):
        here = pl.ds(pl.multiple_of(b * rows, rows), rows)
        more = b + 1 < batches
        q = b * PIECES

        def multiply(j, part):
            source = source_of(j)
            if part == 0:
                for h in range(PIECES):
                    pair_copy(q + h, source, 1 - core).wait_recv()
                x = jnp.zeros((rows, LANES), jnp.float32)
                for t in range(wide_cols // LANES):
                    v = gathered[source, here, t * LANES:(t + 1) * LANES].astype(jnp.float32)
                    x = x + v * v
                if j == 0:
                    squares[...] = x
                else:
                    squares[...] += x
            for p in range(part * half, (part + 1) * half):
                prod = jnp.dot(gathered[source, here, :], mats[p, source], preferred_element_type=jnp.float32)
                prod = prod * scales[p:p + 1, :] * weight_ref[here, p:p + 1]
                if j == 0 and p == 0:
                    total[...] = prod
                else:
                    total[...] += prod

        for j in range(chips):
            last = j == chips - 1

            @pl.when(jnp.logical_and(first_site, b == 0))
            def _():
                spread(j)

            if not last:
                arrive(q, j + 1)
            else:
                @pl.when(jnp.logical_and(more, jnp.logical_not(at_end)))
                def _():
                    own(q + PIECES)
            multiply(j, 0)
            if not last:
                for h in range(1, PIECES):
                    arrive(q + h, j + 1)
            if j == chips - 2:
                @pl.when(jnp.logical_and(more, at_end))
                def _():
                    own(q + PIECES)
            multiply(j, 1)
        norm = jnp.sqrt(jnp.sum(squares[...], axis=1, keepdims=True) / chi + 1e-06)
        inverse = 1.0 / norm
        for h in range(PIECES):
            part = slice(h * piece, (h + 1) * piece)
            leave_ref[pl.ds(pl.multiple_of((q + h) * piece, piece), piece), :] = (
                total[part] * inverse[part]).astype(jnp.bfloat16)

            @pl.when(has_next)
            def _():
                site_copy(q + h).start()

        @pl.when(more)
        def _():
            @pl.when(jnp.logical_not(at_end))
            def _():
                for h in range(1, PIECES):
                    own(q + PIECES + h)

            @pl.when(at_end)
            def _():
                for h in range(1, PIECES):
                    own(q + PIECES + h)
        logs = jnp.transpose(jnp.broadcast_to(jnp.log(norm), (rows, rows)))
        log_ref[0:1, here] = logs[0:1, :]
        return carry

    lax.fori_loop(0, batches, batch, 0)

    def drain(q, carry):
        @pl.when(has_next)
        def _():
            site_copy(q).wait_send()
        for source in range(chips):
            pair_copy(q, source, core).wait_send()

            @pl.when(jnp.logical_and(has_up, source <= chip))
            def _():
                up_copy(q, source).wait_send()

            @pl.when(jnp.logical_and(has_down, source >= chip))
            def _():
                down_copy(q, source).wait_send()
        return carry

    lax.fori_loop(0, batches * PIECES, drain, 0)


def local(start_rows, site_tensors, block_scales, displacement, outcomes):
    sites = lax.axis_size("site")
    bond = lax.axis_size("bond")
    _, chi, phys, cols = site_tensors.shape
    allrows = start_rows.shape[0]
    rows = min(ROWS, allrows)
    pieces = allrows // rows * PIECES
    chips = bond // 2
    chunk = min(CHUNK, 2 * cols)
    slots = min(SLOTS, 2 * cols // chunk)
    sems = pltpu.SemaphoreType.DMA
    vmem = pl.BlockSpec(memory_space=pltpu.VMEM)
    leave, logs = pl.pallas_call(
        functools.partial(kernel, sites, bond),
        out_shape=(jax.ShapeDtypeStruct((allrows, cols), jnp.bfloat16),
                   jax.ShapeDtypeStruct((1, allrows), jnp.float32)),
        in_specs=[pl.BlockSpec(memory_space=pl.ANY), pl.BlockSpec(memory_space=pl.ANY),
                  pl.BlockSpec(memory_space=pltpu.SMEM), vmem, vmem],
        out_specs=(vmem, vmem),
        scratch_shapes=[
            pltpu.VMEM((phys, chips, 2 * cols, cols), jnp.bfloat16),
            pltpu.VMEM((chips, allrows, 2 * cols), jnp.bfloat16),
            pltpu.VMEM((slots, chunk, phys, cols), jnp.bfloat16),
            pltpu.VMEM((cols // LANES, chunk * phys, LANES), jnp.float32),
            pltpu.VMEM((rows, cols), jnp.float32),
            pltpu.VMEM((rows, LANES), jnp.float32),
            pltpu.VMEM((allrows, phys), jnp.float32),
            pltpu.VMEM((phys, cols), jnp.float32),
            sems(()), sems((slots,)),
            sems((pieces, chips)), sems((pieces, chips)), sems((pieces, chips)), sems((pieces,)),
            sems((pieces, chips)), sems((pieces, chips)), sems((pieces,)),
        ],
        compiler_params=pltpu.CompilerParams(
            collective_id=0, has_side_effects=True, vmem_limit_bytes=64000000),
    )(start_rows, site_tensors[0], block_scales[0].T, displacement[0], outcomes)
    return leave[None], logs


def solution(mesh):
    return jax.shard_map(
        local,
        mesh=mesh,
        in_specs=(
            P(None, "bond"),
            P("site", None, None, "bond"),
            P("site", None, "bond"),
            P("site", None, None),
            P("site", None),
        ),
        out_specs=(P("site", None, "bond"), P("site", None)),
        check_vma=False,
    )
```

time: 219 us -> 180 us (0.82)
  Pallas kernels: 210 us -> 176 us
  other arithmetic: 3.31 us -> 0 us
    pallas_call x1, Pallas kernels: 210 us -> 176 us  [local(): pl.pallas_call(functools.partial(kernel, sites, bond), out_shape=(jax.Sha...]
where the time goes in v1:
time: 180 us
  Pallas kernels  176 us (98%)
  local copies, waits for them, and re-layouts  3.53 us (2%)
    pallas_call x1, Pallas kernels, local(): pl.pallas_call(functools.partial(kernel, sites, bond), out_shape=(jax.Sha...  176 us

profile of v1, /device:TPU:7, one launch (start us, length us, event | category | flops | bytes accessed | tf_op | source)
XLA Modules:
  0.0 180.2 jit_solution(752648665488034500)
XLA Ops:
  0.6 176.0 %shard_map.68 = (bf16[1024,512]{1,0:T(8,128)(2,1)}, f32[1,1024]{1,0:T(1,128)}) custom-call(bf16[1024,512]{1,0:T(8,128)(2,1)} %start_hbm.1, bf16[4096,8,512]{2,1,0:T(8,128)(2,1)} %bitcast.6, f32[4,8]{1,0:T(4,128)} %bitcast.9, f32[8,8]{1,0:T(8,128)} %bitcast.8, s32[1,1024]{1,0:T(1,128)} %outcome_ref.1), custom_call_target="tpu_custom_call" | custom-call | tf_op jit(solution)/shard_map/pallas_call | solution.py:312
  176.6 2.3 %copy.9 = bf16[1,1024,512]{2,1,0:T(8,128)(2,1)} copy(bf16[1,1024,512]{2,1,0:T(8,128)(2,1)} %bitcast.7) | data formatting | bytes 2097152
  178.9 1.3 copy.10

commit v2 on v1

--- a/solution.py
+++ b/solution.py
@@ -8,6 +8,10 @@
 
 ROWS = 128
 PIECES = 2
+AHEAD_FIRST = 1
+AHEAD = 1
+OWN_FIRST = 1
+OWN_LATER = 3
 CHUNK = 64
 SLOTS = 8
 LANES = 128
@@ -33,7 +37,6 @@
     pair = me + 1 - 2 * core
     has_up = chip < chips - 1
     has_down = chip > 0
-    at_end = jnp.logical_or(chip == 0, chip == chips - 1)
     first_site = site == 0
     later_site = site > 0
     has_next = site < sites - 1
@@ -200,80 +203,80 @@
         for h in range(PIECES):
             own(h)
 
+    pieces = batches * PIECES
     half = phys // 2
 
-    def batch(b, carry):
+    def multiply(b, j, part):
         here = pl.ds(pl.multiple_of(b * rows, rows), rows)
-        more = b + 1 < batches
-        q = b * PIECES
-
-        def multiply(j, part):
-            source = source_of(j)
-            if part == 0:
-                for h in range(PIECES):
-                    pair_copy(q + h, source, 1 - core).wait_recv()
-                x = jnp.zeros((rows, LANES), jnp.float32)
-                for t in range(wide_cols // LANES):
-                    v = gathered[source, here, t * LANES:(t + 1) * LANES].astype(jnp.float32)
-                    x = x + v * v
-                if j == 0:
-                    squares[...] = x
-                else:
-                    squares[...] += x
-            for p in range(part * half, (part + 1) * half):
-                prod = jnp.dot(gathered[source, here, :], mats[p, source], preferred_element_type=jnp.float32)
-                prod = prod * scales[p:p + 1, :] * weight_ref[here, p:p + 1]
-                if j == 0 and p == 0:
-                    total[...] = prod
-                else:
-                    total[...] += prod
-
-        for j in range(chips):
-            last = j == chips - 1
-
-            @pl.when(jnp.logical_and(first_site, b == 0))
-            def _():
-                spread(j)
-
-            if not last:
-                arrive(q, j + 1)
+        source = source_of(j)
+        if part == 0:
+            for h in range(PIECES):
+                pair_copy(b * PIECES + h, source, 1 - core).wait_recv()
+            x = jnp.zeros((rows, LANES), jnp.float32)
+            for t in range(wide_cols // LANES):
+                v = gathered[source, here, t * LANES:(t + 1) * LANES].astype(jnp.float32)
+                x = x + v * v
+            if j == 0:
+                squares[...] = x
             else:
-                @pl.when(jnp.logical_and(more, jnp.logical_not(at_end)))
-                def _():
-                    own(q + PIECES)
-            multiply(j, 0)
-            if not last:
-                for h in range(1, PIECES):
-                    arrive(q + h, j + 1)
-            if j == chips - 2:
-                @pl.when(jnp.logical_and(more, at_end))
-                def _():
-                    own(q + PIECES)
-            multiply(j, 1)
+                squares[...] += x
+        for p in range(part * half, (part + 1) * half):
+            prod = jnp.dot(gathered[source, here, :], mats[p, source], preferred_element_type=jnp.float32)
+            prod = prod * scales[p:p + 1, :] * weight_ref[here, p:p + 1]
+            if j == 0 and p == 0:
+                total[...] = prod
+            else:
+                total[...] += prod
+
+    def finish(b):
+        here = pl.ds(pl.multiple_of(b * rows, rows), rows)
         norm = jnp.sqrt(jnp.sum(squares[...], axis=1, keepdims=True) / chi + 1e-06)
         inverse = 1.0 / norm
         for h in range(PIECES):
             part = slice(h * piece, (h + 1) * piece)
-            leave_ref[pl.ds(pl.multiple_of((q + h) * piece, piece), piece), :] = (
+            q = b * PIECES + h
+            leave_ref[pl.ds(pl.multiple_of(q * piece, piece), piece), :] = (
                 total[part] * inverse[part]).astype(jnp.bfloat16)
 
             @pl.when(has_next)
             def _():
-                site_copy(q + h).start()
-
-        @pl.when(more)
-        def _():
-            @pl.when(jnp.logical_not(at_end))
-            def _():
-                for h in range(1, PIECES):
-                    own(q + PIECES + h)
-
-            @pl.when(at_end)
-            def _():
-                for h in range(1, PIECES):
-                    own(q + PIECES + h)
+                site_copy(q).start()
         logs = jnp.transpose(jnp.broadcast_to(jnp.log(norm), (rows, rows)))
         log_ref[0:1, here] = logs[0:1, :]
+
+    def batch(b, carry):
+        q = b * PIECES
+        more = b + 1 < batches
+        events = [(hop, h) for hop in range(1, chips) for h in range(PIECES)]
+
+        def handle(upto):
+            while events and len(events) > PIECES * (chips - 1) - upto:
+                hop, h = events.pop(0)
+                arrive(q + h, hop)
+
+        def own_next(hs, here):
+            @pl.when(jnp.logical_and(more, here))
+            def _():
+                for h in hs:
+                    own(q + PIECES + h)
+
+        for j in range(chips):
+            @pl.when(jnp.logical_and(first_site, b == 0))
+            def _():
+                spread(j)
+            for part in range(2):
+                if j == chips - 1:
+                    handle(PIECES * j)
+                elif part == 0:
+                    handle(PIECES * j + (AHEAD_FIRST if j == 0 else AHEAD))
+                else:
+                    handle(PIECES * j + (PIECES if j == 0 else 2 * AHEAD))
+                if 2 * j + part == min(OWN_FIRST, 2 * chips - 1):
+                    own_next(range(PIECES), first_site)
+                if 2 * j + part == min(OWN_LATER, 2 * chips - 1):
+                    own_next(range(PIECES), later_site)
+                multiply(b, j, part)
+        finish(b)
         return carry
 
     lax.fori_loop(0, batches, batch, 0)
@@ -294,7 +297,7 @@
                 down_copy(q, source).wait_send()
         return carry
 
-    lax.fori_loop(0, batches * PIECES, drain, 0)
+    lax.fori_loop(0, pieces, drain, 0)
 
 
 def local(start_rows, site_tensors, block_scales, displacement, outcomes):

time: 180 us -> 159 us (0.88)
  Pallas kernels: 176 us -> 154 us
    pallas_call x1, Pallas kernels: 176 us -> 154 us  [local(): pl.pallas_call(functools.partial(kernel, sites, bond), out_shape=(jax.Sha...]
where the time goes in v2:
time: 159 us; the launch traced here: 158 us
  Pallas kernels  154 us (97%)
  local copies, waits for them, and re-layouts  3.53 us (2%)
    pallas_call x1, Pallas kernels, local(): pl.pallas_call(functools.partial(kernel, sites, bond), out_shape=(jax.Sha...  154 us
    unnamed x2, local copies, waits for them, and re-layouts  3.53 us

profile of v2, /device:TPU:7, one launch (start us, length us, event | category | flops | bytes accessed | tf_op | source)
XLA Modules:
  0.0 158.3 jit_solution(1891695404793193142)
XLA Ops:
  0.6 154.2 %shard_map.68 = (bf16[1024,512]{1,0:T(8,128)(2,1)}, f32[1,1024]{1,0:T(1,128)}) custom-call(bf16[1024,512]{1,0:T(8,128)(2,1)} %start_hbm.1, bf16[4096,8,512]{2,1,0:T(8,128)(2,1)} %bitcast.6, f32[4,8]{1,0:T(4,128)} %bitcast.9, f32[8,8]{1,0:T(8,128)} %bitcast.8, s32[1,1024]{1,0:T(1,128)} %outcome_ref.1), custom_call_target="tpu_custom_call" | custom-call | tf_op jit(solution)/shard_map/pallas_call | solution.py:315
  154.8 2.3 %copy.9 = bf16[1,1024,512]{2,1,0:T(8,128)(2,1)} copy(bf16[1,1024,512]{2,1,0:T(8,128)(2,1)} %bitcast.7) | data formatting | bytes 2097152
  157.1 1.3 copy.10

commit v3 on v2

--- a/solution.py
+++ b/solution.py
@@ -38,6 +38,7 @@
     has_up = chip < chips - 1
     has_down = chip > 0
     first_site = site == 0
+    at_end = jnp.logical_or(chip == 0, chip == chips - 1)
     later_site = site > 0
     has_next = site < sites - 1
 
@@ -171,7 +172,7 @@
             weight = jnp.where(column == o, disp_ref[o:o + 1, :], weight)
         weight_ref[b * rows:(b + 1) * rows, :] = weight
 
-    def spread(j):
+    def spread(j, first, end):
         source = source_of(j)
 
         def step(i, carry):
@@ -194,16 +195,30 @@
                     load(j + 1, i + slots - per_source, slot).start()
             return carry
 
-        lax.fori_loop(0, per_source, step, 0)
+        lax.fori_loop(first, end, step, 0)
 
     @pl.when(later_site)
     def _():
         for j in range(chips):
-            spread(j)
+            spread(j, 0, per_source)
         for h in range(PIECES):
             own(h)
 
     pieces = batches * PIECES
+    ahead = first_site.astype(jnp.int32)
+
+    @pl.when(first_site)
+    def _():
+        for j in range(chips):
+            for h in range(PIECES):
+                spread(j, h * per_source // PIECES, (h + 1) * per_source // PIECES)
+                if j + 1 < chips:
+                    arrive(h, j + 1)
+                if j >= 2 and batches > 1:
+                    arrive(PIECES + h, j - 1)
+            if j in (0, 2) and batches > j // 2 + 1:
+                for h in range(PIECES):
+                    own((j // 2 + 1) * PIECES + h)
     half = phys // 2
 
     def multiply(b, j, part):
@@ -246,24 +261,29 @@
 
     def batch(b, carry):
         q = b * PIECES
-        more = b + 1 < batches
         events = [(hop, h) for hop in range(1, chips) for h in range(PIECES)]
+        begun = jnp.logical_and(first_site, b == 0)
 
         def handle(upto):
             while events and len(events) > PIECES * (chips - 1) - upto:
                 hop, h = events.pop(0)
-                arrive(q + h, hop)
-
-        def own_next(hs, here):
-            @pl.when(jnp.logical_and(more, here))
-            def _():
-                for h in hs:
-                    own(q + PIECES + h)
+                due = b + ahead < batches
+                if hop <= chips - 2:
+                    due = jnp.logical_and(due, jnp.logical_not(begun))
+
+                @pl.when(due)
+                def _():
+                    arrive(q + ahead * PIECES + h, hop)
+
+        def own_next(later, here):
+            due = jnp.logical_and(here, b + later < batches)
+
+            @pl.when(jnp.logical_and(due, jnp.logical_not(begun)))
+            def _():
+                for h in range(PIECES):
+                    own(q + later * PIECES + h)
 
         for j in range(chips):
-            @pl.when(jnp.logical_and(first_site, b == 0))
-            def _():
-                spread(j)
             for part in range(2):
                 if j == chips - 1:
                     handle(PIECES * j)
@@ -272,9 +292,11 @@
                 else:
                     handle(PIECES * j + (PIECES if j == 0 else 2 * AHEAD))
                 if 2 * j + part == min(OWN_FIRST, 2 * chips - 1):
-                    own_next(range(PIECES), first_site)
-                if 2 * j + part == min(OWN_LATER, 2 * chips - 1):
-                    own_next(range(PIECES), later_site)
+                    own_next(2, first_site)
+                if 2 * j + part == 1:
+                    own_next(1, jnp.logical_and(later_site, at_end))
+                if 2 * j + part == 3:
+                    own_next(1, jnp.logical_and(later_site, jnp.logical_not(at_end)))
                 multiply(b, j, part)
         finish(b)
         return carry

time: 159 us -> 158 us (level)
  no operation moved by 1% of the time
where the time goes in v3:
time: 158 us; the launch traced here: 157 us
  Pallas kernels  153 us (97%)
  local copies, waits for them, and re-layouts  3.53 us (2%)
    pallas_call x1, Pallas kernels, local(): pl.pallas_call(functools.partial(kernel, sites, bond), out_shape=(jax.Sha...  153 us
    unnamed x2, local copies, waits for them, and re-layouts  3.53 us

profile of v3, /device:TPU:7, one launch (start us, length us, event | category | flops | bytes accessed | tf_op | source)
XLA Modules:
  0.0 157.5 jit_solution(10751375648456780735)
XLA Ops:
  0.6 153.3 %shard_map.68 = (bf16[1024,512]{1,0:T(8,128)(2,1)}, f32[1,1024]{1,0:T(1,128)}) custom-call(bf16[1024,512]{1,0:T(8,128)(2,1)} %start_hbm.1, bf16[4096,8,512]{2,1,0:T(8,128)(2,1)} %bitcast.6, f32[4,8]{1,0:T(4,128)} %bitcast.9, f32[8,8]{1,0:T(8,128)} %bitcast.8, s32[1,1024]{1,0:T(1,128)} %outcome_ref.1), custom_call_target="tpu_custom_call" | custom-call | tf_op jit(solution)/shard_map/pallas_call | solution.py:337
  153.9 2.3 %copy.9 = bf16[1,1024,512]{2,1,0:T(8,128)(2,1)} copy(bf16[1,1024,512]{2,1,0:T(8,128)(2,1)} %bitcast.7) | data formatting | bytes 2097152
  156.2 1.3 copy.10
